TPU v7x, 32 devices: a whole 2x2x4 slice. The times are simulated.
32 devices in a mesh: fsdp: 16 (over z, x, core), seq: 2 (over y).
Axes of the slice: x: 2, y: 2, z: 4, core: 2. Of those that a mesh axis runs over, the one named last changes fastest.
Arguments:
- inputs: bfloat16 [64, 1104, 512], P('fsdp', 'seq'), may hold values from -6 to 6
- skip_input: bfloat16 [64, 1104, 512], P('fsdp', 'seq'), may hold values from -6 to 6
- cotangent: bfloat16 [64, 1104, 512], P('fsdp', 'seq'), may hold values from -6 to 6
- text_len: int32 [64], P('fsdp'), may hold values from 1 to 79, as said below
- batch_valid: int32 [16, 4], P('fsdp'), may hold values 0 or 1
- skip_weight: bfloat16 [1024, 512], P(('fsdp', 'seq')), may hold values from -0.1875 to 0.1875
- skip_bias: bfloat16 [512], P(('fsdp', 'seq')), may hold values from -3 to 3
- first_gain: bfloat16 [512], P(('fsdp', 'seq')), may hold values from 0.099609375 to 1.8984375
- first_shift: bfloat16 [512], P(('fsdp', 'seq')), may hold values from -3 to 3
- qkv_weight: bfloat16 [512, 1536], P(('fsdp', 'seq')), may hold values from -0.25 to 0.25
- proj_weight: bfloat16 [512, 512], P(('fsdp', 'seq')), may hold values from -3 to 3
- proj_bias: bfloat16 [512], P(('fsdp', 'seq')), may hold values from -3 to 3
- second_gain: bfloat16 [512], P(('fsdp', 'seq')), may hold values from 0.099609375 to 1.8984375
- second_shift: bfloat16 [512], P(('fsdp', 'seq')), may hold values from -3 to 3
- up_weight: bfloat16 [512, 2048], P(('fsdp', 'seq')), may hold values from -0.25 to 0.25
- up_bias: bfloat16 [2048], P(('fsdp', 'seq')), may hold values from -3 to 3
- down_weight: bfloat16 [2048, 512], P(('fsdp', 'seq')), may hold values from -0.125 to 0.125
- down_bias: bfloat16 [512], P(('fsdp', 'seq')), may hold values from -3 to 3
Outputs:
- output: bfloat16 [64, 1104, 512], P('fsdp', 'seq')
- input_grad: bfloat16 [64, 1104, 512], P('fsdp', 'seq')
- skip_grad: bfloat16 [64, 1104, 512], P('fsdp', 'seq')
- skip_weight_grad: float32 [1024, 512], P(('fsdp', 'seq'))
- skip_bias_grad: float32 [512], P(('fsdp', 'seq'))
- first_gain_grad: float32 [512], P(('fsdp', 'seq'))
- first_shift_grad: float32 [512], P(('fsdp', 'seq'))
- qkv_weight_grad: float32 [512, 1536], P(('fsdp', 'seq'))
- proj_weight_grad: float32 [512, 512], P(('fsdp', 'seq'))
- proj_bias_grad: float32 [512], P(('fsdp', 'seq'))
- second_gain_grad: float32 [512], P(('fsdp', 'seq'))
- second_shift_grad: float32 [512], P(('fsdp', 'seq'))
- up_weight_grad: float32 [512, 2048], P(('fsdp', 'seq'))
- up_bias_grad: float32 [2048], P(('fsdp', 'seq'))
- down_weight_grad: float32 [2048, 512], P(('fsdp', 'seq'))
- down_bias_grad: float32 [512], P(('fsdp', 'seq'))
Inputs may be any that keep to these rules, and one draw needn't show every extreme that they name: `text_len`: the number of the text slots of a sequence that are real; the others are padding. `batch_valid`: 1 marks a micro-batch of a group whose sequences count, 0 one whose sequences are padding.
All inputs are finite; a program needn't handle non-finite values.
Results may differ from a plain program's by a relative error of at most 0.014.
Values may be sent and summed in bfloat16 or wider, within the bound.
No kernel may reach another device: no remote copies, remote signals or barrier semaphores. Data moves between devices by JAX's collectives and lax.ppermute only.
A program may use at most 192 MiB of HBM per device.

v0:
```python
import jax
import jax.numpy as jnp
from jax import lax
from jax.sharding import PartitionSpec as P

HEAD_DIM = 64
PATCHES = 1024
MICRO = 4


NEG_BIG = -1e30
EPSILON = 1e-05
heads_per_group = 4


def row_contract(left, right):
    return lax.dot_general(
        left, right, (((0,), (0,)), ((), ())), preferred_element_type=jnp.float32
    )


def column_contract(left, right):
    return lax.dot_general(
        left, right, (((1,), (1,)), ((), ())), preferred_element_type=jnp.float32
    )


def normalize(hidden, gain, shift):
    average = jnp.mean(hidden, axis=-1, keepdims=True)
    centred = hidden - average
    spread = jnp.mean(centred * centred, axis=-1, keepdims=True)
    return centred * lax.rsqrt(spread + EPSILON) * gain + shift


def gelu_exact(value):
    return jax.nn.gelu(value, approximate=False)


def head_slice(array, head_group):
    group_width = heads_per_group * HEAD_DIM
    part = lax.dynamic_slice_in_dim(array, head_group * group_width, group_width, 2)
    return part.reshape(array.shape[0], array.shape[1], heads_per_group, HEAD_DIM)


def restack(stacked):
    seq_count, length = (stacked.shape[1], stacked.shape[2])
    return jnp.transpose(stacked, (1, 2, 0, 3)).reshape(
        seq_count, length, stacked.shape[0] * stacked.shape[3]
    )


def stats_to_rows(stats):
    groups, seq_count, head_count, length = stats.shape
    return jnp.transpose(stats, (1, 3, 0, 2)).reshape(seq_count, length, groups * head_count)


def rows_to_stats(rows, groups):
    seq_count, length = (rows.shape[0], rows.shape[1])
    return jnp.transpose(rows.reshape(seq_count, length, groups, heads_per_group), (2, 0, 3, 1))


def masked_scores(query_part, key_part, allowed, score_scale):
    scores = (
        jnp.einsum("sqhd,skhd->shqk", query_part, key_part, preferred_element_type=jnp.float32)
        * score_scale
    )
    return jnp.where(allowed[:, None, None, :], scores, NEG_BIG)


def attend_forward(queries, keys_all, values_all, allowed, score_scale):
    groups = queries.shape[2] // (heads_per_group * HEAD_DIM)

    def one_group(head_group):
        query_part = head_slice(queries, head_group)
        key_part = head_slice(keys_all, head_group)
        value_part = head_slice(values_all, head_group)
        scores = masked_scores(query_part, key_part, allowed, score_scale)
        row_max = jnp.max(scores, axis=-1, keepdims=True)
        exponent = jnp.exp(scores - row_max)
        row_total = jnp.sum(exponent, axis=-1, keepdims=True)
        softened = (exponent / row_total).astype(jnp.bfloat16)
        mixture = jnp.einsum(
            "shqk,skhd->sqhd", softened, value_part, preferred_element_type=jnp.float32
        )
        logsum = (row_max + jnp.log(row_total))[..., 0]
        return (
            mixture.reshape(mixture.shape[0], mixture.shape[1], heads_per_group * HEAD_DIM),
            logsum,
        )

    mixtures, logsums = lax.map(one_group, jnp.arange(groups))
    return (restack(mixtures), logsums)


def attend_query_side(queries, keys_all, values_all, grad_mixture, logsums, allowed, score_scale):
    groups = queries.shape[2] // (heads_per_group * HEAD_DIM)

    def one_group(sliced):
        head_group, logsum = sliced
        query_part = head_slice(queries, head_group)
        key_part = head_slice(keys_all, head_group)
        value_part = head_slice(values_all, head_group)
        grad_part = head_slice(grad_mixture, head_group)
        scores = masked_scores(query_part, key_part, allowed, score_scale)
        softened = jnp.exp(scores - logsum[..., None])
        prob_grad = jnp.einsum(
            "sqhd,skhd->shqk", grad_part, value_part, preferred_element_type=jnp.float32
        )
        row_inner = jnp.sum(prob_grad * softened, axis=-1, keepdims=True)
        score_grad = (softened * (prob_grad - row_inner)).astype(jnp.bfloat16)
        query_grad = (
            jnp.einsum("shqk,skhd->sqhd", score_grad, key_part, preferred_element_type=jnp.float32)
            * score_scale
        )
        group_width = heads_per_group * HEAD_DIM
        return (
            query_grad.reshape(query_grad.shape[0], query_grad.shape[1], group_width),
            row_inner[..., 0],
        )

    query_grads, inners = lax.map(one_group, (jnp.arange(groups), logsums))
    return (restack(query_grads), inners)


def attend_key_side(
    queries_all,
    keys_here,
    values_here,
    grad_all,
    logsums_all,
    inners_all,
    allowed_here,
    score_scale,
):
    groups = keys_here.shape[2] // (heads_per_group * HEAD_DIM)

    def one_group(sliced):
        head_group, logsum, inner = sliced
        query_part = head_slice(queries_all, head_group)
        key_part = head_slice(keys_here, head_group)
        value_part = head_slice(values_here, head_group)
        grad_part = head_slice(grad_all, head_group)
        scores = masked_scores(query_part, key_part, allowed_here, score_scale)
        softened = jnp.exp(scores - logsum[..., None])
        softened_low = softened.astype(jnp.bfloat16)
        value_grad = jnp.einsum(
            "shqk,sqhd->skhd", softened_low, grad_part, preferred_element_type=jnp.float32
        )
        prob_grad = jnp.einsum(
            "sqhd,skhd->shqk", grad_part, value_part, preferred_element_type=jnp.float32
        )
        score_grad = (softened * (prob_grad - inner[..., None])).astype(jnp.bfloat16)
        key_grad = (
            jnp.einsum(
                "shqk,sqhd->skhd", score_grad, query_part, preferred_element_type=jnp.float32
            )
            * score_scale
        )
        group_width = heads_per_group * HEAD_DIM
        return (
            key_grad.reshape(key_grad.shape[0], key_grad.shape[1], group_width),
            value_grad.reshape(value_grad.shape[0], value_grad.shape[1], group_width),
        )

    key_grads, value_grads = lax.map(one_group, (jnp.arange(groups), logsums_all, inners_all))
    return (restack(key_grads), restack(value_grads))


def local(
    inputs,
    skip_input,
    cotangent,
    text_len,
    batch_valid,
    skip_weight,
    skip_bias,
    first_gain,
    first_shift,
    qkv_weight,
    proj_weight,
    proj_bias,
    second_gain,
    second_shift,
    up_weight,
    up_bias,
    down_weight,
    down_bias,
):
    local_length = inputs.shape[1]
    model_width = inputs.shape[2]
    full_length = local_length * lax.axis_size("seq")
    per_batch = inputs.shape[0] // MICRO
    rows_here = per_batch * local_length
    score_scale = HEAD_DIM ** (-0.5)
    groups = model_width // (heads_per_group * HEAD_DIM)
    key_position = jnp.arange(full_length, dtype=jnp.int32)
    local_position = lax.axis_index("seq") * local_length + jnp.arange(
        local_length, dtype=jnp.int32
    )
    totals = None
    outputs, input_grads, skip_grads = ([], [], [])
    for micro_batch in range(MICRO):
        first_row = micro_batch * per_batch
        last_row = first_row + per_batch
        params = (
            lax.all_gather(skip_weight, ("fsdp", "seq"), axis=0, tiled=True),
            lax.all_gather(skip_bias, ("fsdp", "seq"), axis=0, tiled=True),
            lax.all_gather(first_gain, ("fsdp", "seq"), axis=0, tiled=True),
            lax.all_gather(first_shift, ("fsdp", "seq"), axis=0, tiled=True),
            lax.all_gather(qkv_weight, ("fsdp", "seq"), axis=0, tiled=True),
            lax.all_gather(proj_weight, ("fsdp", "seq"), axis=0, tiled=True),
            lax.all_gather(proj_bias, ("fsdp", "seq"), axis=0, tiled=True),
            lax.all_gather(second_gain, ("fsdp", "seq"), axis=0, tiled=True),
            lax.all_gather(second_shift, ("fsdp", "seq"), axis=0, tiled=True),
            lax.all_gather(up_weight, ("fsdp", "seq"), axis=0, tiled=True),
            lax.all_gather(up_bias, ("fsdp", "seq"), axis=0, tiled=True),
            lax.all_gather(down_weight, ("fsdp", "seq"), axis=0, tiled=True),
            lax.all_gather(down_bias, ("fsdp", "seq"), axis=0, tiled=True),
        )
        (
            skip_matrix,
            skip_offset,
            gain_one,
            shift_one,
            qkv_matrix,
            proj_matrix,
            proj_offset,
            gain_two,
            shift_two,
            up_matrix,
            up_offset,
            down_matrix,
            down_offset,
        ) = params
        joined = jnp.concatenate(
            [inputs[first_row:last_row], skip_input[first_row:last_row]], axis=2
        ).reshape(rows_here, 2 * model_width)
        stream_first = jnp.dot(
            joined, skip_matrix, preferred_element_type=jnp.float32
        ) + skip_offset.astype(jnp.float32)
        normed_first, back_first = jax.vjp(
            normalize, stream_first, gain_one.astype(jnp.float32), shift_one.astype(jnp.float32)
        )
        attn_in = normed_first.astype(jnp.bfloat16)
        qkv_low = jnp.dot(attn_in, qkv_matrix, preferred_element_type=jnp.float32).astype(
            jnp.bfloat16
        )
        qkv_low = qkv_low.reshape(per_batch, local_length, 3 * model_width)
        queries = qkv_low[..., :model_width]
        keys_here = qkv_low[..., model_width : 2 * model_width]
        values_here = qkv_low[..., 2 * model_width :]
        keys_all, values_all = (
            lax.all_gather(keys_here, "seq", axis=1, tiled=True),
            lax.all_gather(values_here, "seq", axis=1, tiled=True),
        )
        limits = (PATCHES + 1 + text_len[first_row:last_row])[:, None]
        allowed = key_position[None, :] < limits
        mixture, logsums = attend_forward(queries, keys_all, values_all, allowed, score_scale)
        mixture_low = mixture.astype(jnp.bfloat16).reshape(rows_here, model_width)
        stream_second = (
            stream_first
            + jnp.dot(mixture_low, proj_matrix, preferred_element_type=jnp.float32)
            + proj_offset.astype(jnp.float32)
        )
        normed_second, back_second = jax.vjp(
            normalize, stream_second, gain_two.astype(jnp.float32), shift_two.astype(jnp.float32)
        )
        mlp_in = normed_second.astype(jnp.bfloat16)
        hidden_pre = jnp.dot(
            mlp_in, up_matrix, preferred_element_type=jnp.float32
        ) + up_offset.astype(jnp.float32)
        activated, back_gelu = jax.vjp(gelu_exact, hidden_pre)
        activated_low = activated.astype(jnp.bfloat16)
        branch = jnp.dot(
            activated_low, down_matrix, preferred_element_type=jnp.float32
        ) + down_offset.astype(jnp.float32)
        validity = batch_valid[0, micro_batch].astype(jnp.float32)
        outputs.append(
            ((stream_second + branch) * validity)
            .astype(jnp.bfloat16)
            .reshape(per_batch, local_length, model_width)
        )
        params = (
            lax.all_gather(skip_weight, ("fsdp", "seq"), axis=0, tiled=True),
            lax.all_gather(skip_bias, ("fsdp", "seq"), axis=0, tiled=True),
            lax.all_gather(first_gain, ("fsdp", "seq"), axis=0, tiled=True),
            lax.all_gather(first_shift, ("fsdp", "seq"), axis=0, tiled=True),
            lax.all_gather(qkv_weight, ("fsdp", "seq"), axis=0, tiled=True),
            lax.all_gather(proj_weight, ("fsdp", "seq"), axis=0, tiled=True),
            lax.all_gather(proj_bias, ("fsdp", "seq"), axis=0, tiled=True),
            lax.all_gather(second_gain, ("fsdp", "seq"), axis=0, tiled=True),
            lax.all_gather(second_shift, ("fsdp", "seq"), axis=0, tiled=True),
            lax.all_gather(up_weight, ("fsdp", "seq"), axis=0, tiled=True),
            lax.all_gather(up_bias, ("fsdp", "seq"), axis=0, tiled=True),
            lax.all_gather(down_weight, ("fsdp", "seq"), axis=0, tiled=True),
            lax.all_gather(down_bias, ("fsdp", "seq"), axis=0, tiled=True),
        )
        (
            skip_matrix,
            skip_offset,
            gain_one,
            shift_one,
            qkv_matrix,
            proj_matrix,
            proj_offset,
            gain_two,
            shift_two,
            up_matrix,
            up_offset,
            down_matrix,
            down_offset,
        ) = params
        grad_out = (
            cotangent[first_row:last_row].reshape(rows_here, model_width).astype(jnp.float32)
            * validity
        )
        grad_branch = grad_out.astype(jnp.bfloat16)
        down_grad = row_contract(activated_low, grad_branch)
        down_offset_grad = jnp.sum(grad_branch.astype(jnp.float32), axis=0)
        grad_act = column_contract(grad_branch, down_matrix)
        (grad_pre,) = back_gelu(grad_act)
        grad_pre_low = grad_pre.astype(jnp.bfloat16)
        up_grad = row_contract(mlp_in, grad_pre_low)
        up_offset_grad = jnp.sum(grad_pre_low.astype(jnp.float32), axis=0)
        grad_mlp_in = column_contract(grad_pre_low, up_matrix)
        norm_term_second, gain_two_grad, shift_two_grad = back_second(grad_mlp_in)
        grad_stream_second = grad_out + norm_term_second
        grad_proj = grad_stream_second.astype(jnp.bfloat16)
        proj_grad = row_contract(mixture_low, grad_proj)
        proj_offset_grad = jnp.sum(grad_proj.astype(jnp.float32), axis=0)
        grad_mixture = (
            column_contract(grad_proj, proj_matrix)
            .astype(jnp.bfloat16)
            .reshape(per_batch, local_length, model_width)
        )
        query_grad, inners = attend_query_side(
            queries, keys_all, values_all, grad_mixture, logsums, allowed, score_scale
        )
        queries_all, grad_all = (
            lax.all_gather(queries, "seq", axis=1, tiled=True),
            lax.all_gather(grad_mixture, "seq", axis=1, tiled=True),
        )
        logsum_rows, inner_rows = (
            lax.all_gather(stats_to_rows(logsums), "seq", axis=1, tiled=True),
            lax.all_gather(stats_to_rows(inners), "seq", axis=1, tiled=True),
        )
        allowed_here = local_position[None, :] < limits
        key_grad, value_grad = attend_key_side(
            queries_all,
            keys_here,
            values_here,
            grad_all,
            rows_to_stats(logsum_rows, groups),
            rows_to_stats(inner_rows, groups),
            allowed_here,
            score_scale,
        )
        grad_qkv = (
            jnp.concatenate([query_grad, key_grad, value_grad], axis=2)
            .astype(jnp.bfloat16)
            .reshape(rows_here, 3 * model_width)
        )
        qkv_grad = row_contract(attn_in, grad_qkv)
        grad_attn_in = column_contract(grad_qkv, qkv_matrix)
        norm_term_first, gain_one_grad, shift_one_grad = back_first(grad_attn_in)
        grad_stream_first = (grad_stream_second + norm_term_first).astype(jnp.bfloat16)
        skip_matrix_grad = row_contract(joined, grad_stream_first)
        skip_offset_grad = jnp.sum(grad_stream_first.astype(jnp.float32), axis=0)
        grad_joined = column_contract(grad_stream_first, skip_matrix).reshape(
            per_batch, local_length, 2 * model_width
        )
        input_grads.append(grad_joined[..., :model_width].astype(jnp.bfloat16))
        skip_grads.append(grad_joined[..., model_width:].astype(jnp.bfloat16))
        step_grads = (
            skip_matrix_grad,
            skip_offset_grad,
            gain_one_grad,
            shift_one_grad,
            qkv_grad,
            proj_grad,
            proj_offset_grad,
            gain_two_grad,
            shift_two_grad,
            up_grad,
            up_offset_grad,
            down_grad,
            down_offset_grad,
        )
        if totals is None:
            totals = tuple(step_grads)
        else:
            totals = jax.tree.map(jnp.add, tuple(totals), tuple(step_grads))
    totals = (
        lax.psum_scatter(totals[0], ("fsdp", "seq"), scatter_dimension=0, tiled=True),
        lax.psum_scatter(totals[1], ("fsdp", "seq"), scatter_dimension=0, tiled=True),
        lax.psum_scatter(totals[2], ("fsdp", "seq"), scatter_dimension=0, tiled=True),
        lax.psum_scatter(totals[3], ("fsdp", "seq"), scatter_dimension=0, tiled=True),
        lax.psum_scatter(totals[4], ("fsdp", "seq"), scatter_dimension=0, tiled=True),
        lax.psum_scatter(totals[5], ("fsdp", "seq"), scatter_dimension=0, tiled=True),
        lax.psum_scatter(totals[6], ("fsdp", "seq"), scatter_dimension=0, tiled=True),
        lax.psum_scatter(totals[7], ("fsdp", "seq"), scatter_dimension=0, tiled=True),
        lax.psum_scatter(totals[8], ("fsdp", "seq"), scatter_dimension=0, tiled=True),
        lax.psum_scatter(totals[9], ("fsdp", "seq"), scatter_dimension=0, tiled=True),
        lax.psum_scatter(totals[10], ("fsdp", "seq"), scatter_dimension=0, tiled=True),
        lax.psum_scatter(totals[11], ("fsdp", "seq"), scatter_dimension=0, tiled=True),
        lax.psum_scatter(totals[12], ("fsdp", "seq"), scatter_dimension=0, tiled=True),
    )
    output = jnp.concatenate(outputs, axis=0)
    input_grad = jnp.concatenate(input_grads, axis=0)
    skip_grad = jnp.concatenate(skip_grads, axis=0)
    return (
        output,
        input_grad,
        skip_grad,
        totals[0],
        totals[1],
        totals[2],
        totals[3],
        totals[4],
        totals[5],
        totals[6],
        totals[7],
        totals[8],
        totals[9],
        totals[10],
        totals[11],
        totals[12],
    )


def solution(mesh):
    return jax.shard_map(
        local,
        mesh=mesh,
        in_specs=(
            P("fsdp", "seq", None),
            P("fsdp", "seq", None),
            P("fsdp", "seq", None),
            P("fsdp"),
            P("fsdp", None),
            P(("fsdp", "seq"), None),
            P(("fsdp", "seq")),
            P(("fsdp", "seq")),
            P(("fsdp", "seq")),
            P(("fsdp", "seq"), None),
            P(("fsdp", "seq"), None),
            P(("fsdp", "seq")),
            P(("fsdp", "seq")),
            P(("fsdp", "seq")),
            P(("fsdp", "seq"), None),
            P(("fsdp", "seq")),
            P(("fsdp", "seq"), None),
            P(("fsdp", "seq")),
        ),
        out_specs=(
            P("fsdp", "seq", None),
            P("fsdp", "seq", None),
            P("fsdp", "seq", None),
            P(("fsdp", "seq"), None),
            P(("fsdp", "seq")),
            P(("fsdp", "seq")),
            P(("fsdp", "seq")),
            P(("fsdp", "seq"), None),
            P(("fsdp", "seq"), None),
            P(("fsdp", "seq")),
            P(("fsdp", "seq")),
            P(("fsdp", "seq")),
            P(("fsdp", "seq"), None),
            P(("fsdp", "seq")),
            P(("fsdp", "seq"), None),
            P(("fsdp", "seq")),
        ),
        check_vma=False,
    )
```

profile of v0, /device:TPU:0, one launch (start us, length us, event | category | flops | bytes accessed | tf_op | source)
XLA Modules:
  0.0 1626.7 jit_solution(15785393731040309564)
XLA Ops:
  15.5 42.2 %all-reduce.17 = (bf16[512]{0:T(512)(128)(2,1)S(1)}, bf16[512]{0:T(512)(128)(2,1)S(1)}, bf16[512]{0:T(512)(128)(2,1)S(1)}, bf16[512]{0:T(512)(128)(2,1)S(1)}, bf...) all-reduce(bf16[512]{0:T(512)(128)(2,1)S(1)} %dynamic-update-slice,, ...), channel_id=1, replica_groups=mesh['fsdp'=16,'seq'=2] {'fsdp','seq'}, use_global_device_ids=true, to_apply=%add | all-reduce | flops 5632 | bytes 22528
  69.9 54.6 %all-gather.27.cloned.1.call-done = bf16[512,1536]{1,0:T(8,128)(2,1)} async-done(((bf16[16,1536]{1,0:T(8,128)(2,1)}), bf16[512,1536]{1,0:T(8,128)(2,1)}) %all-gather.27.cloned.1.call-update) | async-done | bytes 1572880 | tf_op jit(solution)/shard_map/all_gather | solution.py:210
  161.1 70.1 %all_gather.81 = bf16[512,512]{1,0:T(8,128)(2,1)S(1)} all-gather(bf16[16,512]{1,0:T(8,128)(2,1)S(1)} %copy-done.206), channel_id=1, replica_groups=mesh['fsdp'=16,'seq'=2] {'fsdp','seq'}, dimensions={0}, use_global_device_ids=true | all-gather | bytes 540672 | tf_op jit(solution)/shard_map/all_gather | solution.py:211
  241.9 22.4 %while.159 = (s32[]{:T(128)}, bf16[2,1,552,256]{2,3,1,0:T(8,128)(2,1)S(1)}, f32[2,1,4,552]{3,2,1,0:T(4,128)S(1)}, s32[2]{0:T(128)S(1)}, bf16[1,1104,512]{1,2,0:T...) while((s32[]{:T(128)}, ...), condition=%wide.region_29.30_spmd.clone, body=%wide.region_26.29_spmd.clone.sunk | while | flops 653284224 | bytes 34508424 | solution.py:91
  271.7 22.5 %while.158 = (s32[]{:T(128)}, bf16[2,1,552,256]{2,3,1,0:T(8,128)(2,1)S(1)}, f32[2,1,4,552]{3,2,1,0:T(4,128)S(1)}, s32[2]{0:T(128)S(1)}, bf16[1,1104,512]{1,2,0:T...) while((s32[]{:T(128)}, ...), condition=%wide.region_21.22_spmd.clone, body=%wide.region_18.21_spmd.clone.sunk | while | flops 653284224 | bytes 34508424 | solution.py:91
  301.6 22.6 %while.157 = (s32[]{:T(128)}, bf16[2,1,552,256]{2,3,1,0:T(8,128)(2,1)S(1)}, f32[2,1,4,552]{3,2,1,0:T(4,128)S(1)}, s32[2]{0:T(128)S(1)}, bf16[1,1104,512]{1,2,0:T...) while((s32[]{:T(128)}, ...), condition=%wide.region_13.14_spmd.clone, body=%wide.region_10.13_spmd.clone.sunk | while | flops 653284224 | bytes 34508424 | solution.py:91
  332.1 22.8 %while.156 = (s32[]{:T(128)}, bf16[2,1,552,256]{2,3,1,0:T(8,128)(2,1)S(1)}, f32[2,1,4,552]{3,2,1,0:T(4,128)S(1)}, s32[2]{0:T(128)S(1)}, bf16[1,1104,512]{1,2,0:T...) while((s32[]{:T(128)}, ...), condition=%wide.region_5.6_spmd.clone, body=%wide.region_2.5_spmd.clone.sunk | while | flops 653284224 | bytes 34508424 | solution.py:91
  358.9 23.4 %all-gather.33.cloned.1.call-done = bf16[512,2048]{1,0:T(8,128)(2,1)} async-done(((bf16[16,2048]{1,0:T(8,128)(2,1)}), bf16[512,2048]{1,0:T(8,128)(2,1)}) %all-gather.33.cloned.1.call-update) | async-done | bytes 2097168 | tf_op jit(solution)/shard_map/all_gather | solution.py:215
  391.5 47.0 %multiply_convert_fusion.23 = (bf16[552,2048]{1,0:T(8,128)(2,1)}, f32[552,2048]{1,0:T(8,128)}, bf16[552,2048]{1,0:T(8,128)(2,1)}, f32[552,2048]{1,0:T(8,128)}, b...) fusion(f32[2048]{0:T(1024)S(1)} %copy-done.221, ...), kind=kOutput, calls=%fused_computation.275 | convolution fusion | flops 1457491968 | bytes 48464192 | tf_op jit(solution)/shard_map/dot_general | solution.py:269
  440.5 6.7 convert_reduce_fusion
  456.2 6.3 convert_reduce_fusion.2
  484.2 16.1 all_gather.196
  501.8 9.2 all_gather.204
  514.1 52.1 %while.166 = (s32[]{:T(128)}, bf16[2,1,552,256]{2,3,1,0:T(8,128)(2,1)}, f32[2,1,4,552]{3,2,1,0:T(4,128)}, s32[2]{0:T(128)S(1)}, bf16[1,1104,512]{1,2,0:T(8,128)(...) while((s32[]{:T(128)}, ...), condition=%wide.region_63.64_spmd.clone, body=%wide.region_61.63_spmd.clone.sunk | while | flops 963146112 | bytes 86507416 | solution.py:121
  525.9 7.7 multiply_reduce_fusion.35
  551.9 7.6 multiply_reduce_fusion.35
  567.1 15.6 all_gather.206
  584.2 7.9 all_gather.200
  595.2 52.1 %while.164 = (s32[]{:T(128)}, bf16[2,1,552,256]{2,3,1,0:T(8,128)(2,1)}, f32[2,1,4,552]{3,2,1,0:T(4,128)}, s32[2]{0:T(128)S(1)}, bf16[1,1104,512]{1,2,0:T(8,128)(...) while((s32[]{:T(128)}, ...), condition=%wide.region_54.55_spmd.clone, body=%wide.region_52.54_spmd.clone.sunk | while | flops 963146112 | bytes 86507416 | solution.py:121
  607.0 7.6 multiply_reduce_fusion.34
  633.1 7.6 multiply_reduce_fusion.34
  648.2 7.3 all_gather.202
  657.0 7.3 all_gather.192
  667.6 52.1 %while.160 = (s32[]{:T(128)}, bf16[2,1,552,256]{2,3,1,0:T(8,128)(2,1)}, f32[2,1,4,552]{3,2,1,0:T(4,128)}, s32[2]{0:T(128)S(1)}, bf16[1,1104,512]{1,2,0:T(8,128)(...) while((s32[]{:T(128)}, ...), condition=%wide.region_36.37_spmd.clone, body=%wide.region_34.36_spmd.clone.sunk | while | flops 963146112 | bytes 86507416 | solution.py:121
  679.4 7.6 multiply_reduce_fusion.32
  705.4 7.6 multiply_reduce_fusion.32
  720.7 7.3 all_gather.194
  731.9 43.4 %while.167 = (s32[]{:T(128)}, bf16[2,1,552,256]{2,3,1,0:T(8,128)(2,1)}, bf16[2,1,552,256]{2,3,1,0:T(8,128)(2,1)}, s32[2]{0:T(128)S(1)}, bf16[1,1104,512]{2,1,0:T...) while((s32[]{:T(128)}, ...), condition=%wide.region_65.66_spmd.clone, body=%wide.region_64.65_spmd.clone.sunk | while | flops 1272727552 | bytes 79935112 | solution.py:165
  742.7 8.9 fusion.572
  764.4 8.9 fusion.572
  777.0 43.6 %while.165 = (s32[]{:T(128)}, bf16[2,1,552,256]{2,3,1,0:T(8,128)(2,1)}, bf16[2,1,552,256]{2,3,1,0:T(8,128)(2,1)}, s32[2]{0:T(128)S(1)}, bf16[1,1104,512]{2,1,0:T...) while((s32[]{:T(128)}, ...), condition=%wide.region_56.57_spmd.clone, body=%wide.region_55.56_spmd.clone.sunk | while | flops 1272727552 | bytes 82337480 | solution.py:165
  788.1 8.9 fusion.555
  809.8 8.9 fusion.555
  822.5 42.3 %while.161 = (s32[]{:T(128)}, bf16[2,1,552,256]{2,3,1,0:T(8,128)(2,1)}, bf16[2,1,552,256]{2,3,1,0:T(8,128)(2,1)}, s32[2]{0:T(128)S(1)}, bf16[1,1104,512]{2,1,0:T...) while((s32[]{:T(128)}, ...), condition=%wide.region_38.39_spmd.clone, body=%wide.region_37.38_spmd.clone.sunk | while | flops 1272727552 | bytes 80031400 | solution.py:165
  832.8 8.9 fusion.521
  853.6 8.9 fusion.521
  883.3 50.5 %while.162 = (s32[]{:T(128)}, bf16[2,1,552,256]{2,3,1,0:T(8,128)(2,1)}, f32[2,1,4,552]{3,2,1,0:T(4,128)S(1)}, s32[2]{0:T(128)}, bf16[1,1104,512]{1,2,0:T(8,128)(...) while((s32[]{:T(128)}, ...), condition=%wide.region_45.46_spmd.clone, body=%wide.region_43.45_spmd.clone.sunk | while | flops 963146112 | bytes 88769848 | solution.py:121
  895.0 7.6 multiply_reduce_fusion.33
  920.2 7.6 multiply_reduce_fusion.33
  934.0 7.3 all_gather.198
  954.3 42.1 %while.163 = (s32[]{:T(128)}, bf16[2,1,552,256]{2,3,1,0:T(8,128)(2,1)}, bf16[2,1,552,256]{2,3,1,0:T(8,128)(2,1)}, s32[2]{0:T(128)S(1)}, bf16[1,1104,512]{2,1,0:T...) while((s32[]{:T(128)}, ...), condition=%wide.region_47.48_spmd.clone, body=%wide.region_46.47_spmd.clone.sunk | while | flops 1272727552 | bytes 79890056 | solution.py:165
  964.6 8.9 fusion.538
  985.4 8.9 fusion.538
  1059.5 40.9 %all-reduce.16 = (f32[512]{0:T(512)S(1)}, f32[512]{0:T(512)S(1)}, f32[512]{0:T(512)S(1)}, f32[512]{0:T(512)S(1)}, f32[512]{0:T(512)S(1)}, /*index=5*/f32[512]{0:T(512)S(1)}, f32[2048]{0:T(1024)S(1)}, f32[512]{0:T(512)S(1)}) all-reduce(f32[512]{0:T(512)S(1)} %add_add_fusion.18, ...), channel_id=7, replica_groups=mesh['fsdp'=16,'seq'=2] {'fsdp','seq'}, use_global_device_ids=true, to_apply=%region_73.74.clone | all-reduce | flops 5632 | bytes 45056
  1111.4 116.6 %reduce-scatter.6.cloned.1.call-done = f32[32,512]{1,0:T(8,128)} async-done(((f32[1024,512]{1,0:T(8,128)}), f32[32,512]{1,0:T(8,128)}) %reduce-scatter.6.cloned.1.call-update) | async-done | bytes 65552 | tf_op jit(solution)/shard_map/reduce_scatter | solution.py:394
  1228.0 104.4 %reduce-scatter.8.cloned.1.call-done = f32[16,1536]{1,0:T(8,128)} async-done(((f32[512,1536]{1,0:T(8,128)}), f32[16,1536]{1,0:T(8,128)}) %reduce-scatter.8.cloned.1.call-update) | async-done | bytes 98320 | tf_op jit(solution)/shard_map/reduce_scatter | solution.py:398
  1332.4 144.6 %reduce-scatter.12.cloned.1.call-done = f32[16,2048]{1,0:T(8,128)} async-done(((f32[512,2048]{1,0:T(8,128)}), f32[16,2048]{1,0:T(8,128)}) %reduce-scatter.12.cloned.1.call-update) | async-done | bytes 131088 | tf_op jit(solution)/shard_map/reduce_scatter | solution.py:403
  1477.0 143.0 %reduce-scatter.14.cloned.1.call-done = f32[64,512]{1,0:T(8,128)} async-done(((f32[2048,512]{1,0:T(8,128)}), f32[64,512]{1,0:T(8,128)}) %reduce-scatter.14.cloned.1.call-update) | async-done | bytes 131088 | tf_op jit(solution)/shard_map/reduce_scatter | solution.py:405
  (1197 shorter events, 575.0 us)
Async XLA Ops:
  7.2 60.3 %all-gather.25.cloned.1.call-start = ((), (), s32[]{:S(2)}) async-start(), calls=%async_computation.5 | async-start | bytes 1081344 | tf_op jit(solution)/shard_map/all_gather | solution.py:206
  7.9 116.6 %all-gather.27.cloned.1.call-start = ((), (), s32[]{:S(2)}) async-start(), calls=%async_computation.6 | async-start | bytes 1622016 | tf_op jit(solution)/shard_map/all_gather | solution.py:210
  8.7 228.3 %all-gather.45.cloned.1.call-start = ((), (), s32[]{:S(2)}) async-start(), calls=%async_computation.15 | async-start | bytes 1695744 | tf_op jit(solution)/shard_map/all_gather | solution.py:254
  57.8 88.8 %copy-start.238 = (f32[512]{0:T(512)}, f32[512]{0:T(512)S(1)}, u32[]{:S(2)}) copy-start(f32[512]{0:T(512)S(1)} %convert_element_type.394) | copy-start | bytes 6148
  57.8 88.7 %copy-start.189 = (f32[512]{0:T(512)}, f32[512]{0:T(512)S(1)}, u32[]{:S(2)}) copy-start(f32[512]{0:T(512)S(1)} %convert_element_type.393) | copy-start | bytes 6148
  61.7 74.0 %copy-start.106 = (bf16[1,552,512]{2,1,0:T(8,128)(2,1)}, bf16[1,552,512]{2,1,0:T(8,128)(2,1)S(1)}, u32[]{:S(2)}) copy-start(bf16[1,552,512]{2,1,0:T(8,128)(2,1)S(1)} %get-tuple-element.1793) | copy-start | bytes 1695748
  61.7 74.0 %copy-start.108 = (bf16[1,552,512]{2,1,0:T(8,128)(2,1)}, bf16[1,552,512]{2,1,0:T(8,128)(2,1)S(1)}, u32[]{:S(2)}) copy-start(bf16[1,552,512]{2,1,0:T(8,128)(2,1)S(1)} %get-tuple-element.1887) | copy-start | bytes 1695748
  69.5 194.8 %copy-start.39 = (f32[552,512]{1,0:T(8,128)}, f32[552,512]{1,0:T(8,128)S(1)}, u32[]{:S(2)}) copy-start(f32[552,512]{1,0:T(8,128)S(1)} %get-tuple-element.1857) | copy-start | bytes 3391492
  69.5 57.5 %copy-start.151 = (f32[552]{0:T(1024)}, f32[552]{0:T(1024)S(1)}, u32[]{:S(2)}) copy-start(f32[552]{0:T(1024)S(1)} %broadcast_multiply_fusion.1) | copy-start | bytes 6628
  69.8 57.2 %copy-start.175 = (f32[552]{0:T(1024)}, f32[552]{0:T(1024)S(1)}, u32[]{:S(2)}) copy-start(f32[552]{0:T(1024)S(1)} %multiply_reduce_fusion.21) | copy-start | bytes 6628
  69.9 57.2 %copy-start.192 = (f32[552]{0:T(1024)}, f32[552]{0:T(1024)S(1)}, u32[]{:S(2)}) copy-start(f32[552]{0:T(1024)S(1)} %fusion.181) | copy-start | bytes 6628
  128.3 111.1 %all-gather.47.cloned.1.call-start = ((), (), s32[]{:S(2)}) async-start(), calls=%async_computation.16 | async-start | bytes 1695744 | tf_op jit(solution)/shard_map/all_gather | solution.py:253
  130.8 136.1 %all-gather.41.cloned.1.call-start = ((), (), s32[]{:S(2)}) async-start(), calls=%async_computation.13 | async-start | bytes 1695744 | tf_op jit(solution)/shard_map/all_gather | solution.py:254
  135.6 133.6 %all-gather.43.cloned.1.call-start = ((), (), s32[]{:S(2)}) async-start(), calls=%async_computation.14 | async-start | bytes 1695744 | tf_op jit(solution)/shard_map/all_gather | solution.py:253
  137.8 159.0 %all-gather.37.cloned.1.call-start = ((), (), s32[]{:S(2)}) async-start(), calls=%async_computation.11 | async-start | bytes 1695744 | tf_op jit(solution)/shard_map/all_gather | solution.py:254
  143.1 91.5 %copy-start.64 = (bf16[1,552,512]{2,1,0:T(8,128)(2,1)}, bf16[1,552,512]{2,1,0:T(8,128)(2,1)S(1)}, u32[]{:S(2)}) copy-start(bf16[1,552,512]{2,1,0:T(8,128)(2,1)S(1)} %get-tuple-element.1804) | copy-start | bytes 1695748
  143.1 156.1 %all-gather.39.cloned.1.call-start = ((), (), s32[]{:S(2)}) async-start(), calls=%async_computation.12 | async-start | bytes 1695744 | tf_op jit(solution)/shard_map/all_gather | solution.py:253
  145.6 181.6 %all-gather.29.cloned.1.call-start = ((), (), s32[]{:S(2)}) async-start(), calls=%async_computation.7 | async-start | bytes 1695744 | tf_op jit(solution)/shard_map/all_gather | solution.py:254
  150.9 84.8 %copy-start.65 = (bf16[1,552,512]{2,1,0:T(8,128)(2,1)}, bf16[1,552,512]{2,1,0:T(8,128)(2,1)S(1)}, u32[]{:S(2)}) copy-start(bf16[1,552,512]{2,1,0:T(8,128)(2,1)S(1)} %get-tuple-element.1801) | copy-start | bytes 1695748
  150.9 82.6 %copy-start.66 = (bf16[1,552,512]{2,1,0:T(8,128)(2,1)S(1)}, bf16[1,552,512]{2,1,0:T(8,128)(2,1)}, u32[]{:S(2)}) copy-start(bf16[1,552,512]{2,1,0:T(8,128)(2,1)} %get-tuple-element.1807) | copy-start | bytes 1695748
  150.9 178.7 %all-gather.31.cloned.1.call-start = ((), (), s32[]{:S(2)}) async-start(), calls=%async_computation.8 | async-start | bytes 1695744 | tf_op jit(solution)/shard_map/all_gather | solution.py:253
  151.5 230.7 %all-gather.33.cloned.1.call-start = ((), (), s32[]{:S(2)}) async-start(), calls=%async_computation.9 | async-start | bytes 2162688 | tf_op jit(solution)/shard_map/all_gather | solution.py:215
  152.3 288.2 %all-gather.35.cloned.1.call-start = ((), (), s32[]{:S(2)}) async-start(), calls=%async_computation.10 | async-start | bytes 2162688 | tf_op jit(solution)/shard_map/all_gather | solution.py:217
  152.8 577.2 %all-gather.55.cloned.1.call-start = ((), (), s32[]{:S(2)}) async-start(), calls=%async_computation.20 | async-start | bytes 1695744 | tf_op jit(solution)/shard_map/all_gather | solution.py:340
  231.1 124.7 %copy-start.4 = (bf16[512,512]{1,0:T(8,128)(2,1)}, bf16[512,512]{1,0:T(8,128)(2,1)S(1)}, u32[]{:S(2)}) copy-start(bf16[512,512]{1,0:T(8,128)(2,1)S(1)} %all_gather.81) | copy-start | bytes 1572868
  236.8 493.3 %all-gather.63.cloned.1.call-start = ((), (), s32[]{:S(2)}) async-start(), calls=%async_computation.29 | async-start | bytes 1695744 | tf_op jit(solution)/shard_map/all_gather | solution.py:341
  326.8 60.4 %copy-start.11 = (f32[552,512]{1,0:T(8,128)}, f32[552,512]{1,0:T(8,128)S(1)}, u32[]{:S(2)}) copy-start(f32[552,512]{1,0:T(8,128)S(1)} %get-tuple-element.1871) | copy-start | bytes 3391492
  326.9 60.4 %copy-start.138 = (f32[552]{0:T(1024)}, f32[552]{0:T(1024)S(1)}, u32[]{:S(2)}) copy-start(f32[552]{0:T(1024)S(1)} %broadcast_multiply_fusion.4) | copy-start | bytes 6628
  327.2 60.1 %copy-start.146 = (f32[552]{0:T(1024)}, f32[552]{0:T(1024)S(1)}, u32[]{:S(2)}) copy-start(f32[552]{0:T(1024)S(1)} %fusion.178) | copy-start | bytes 6628
  357.9 113.0 %copy-start.14 = (f32[552,512]{1,0:T(8,128)}, f32[552,512]{1,0:T(8,128)S(1)}, u32[]{:S(2)}) copy-start(f32[552,512]{1,0:T(8,128)S(1)} %get-tuple-element.1861) | copy-start | bytes 3391492
  357.9 113.0 %copy-start.141 = (f32[552]{0:T(1024)}, f32[552]{0:T(1024)S(1)}, u32[]{:S(2)}) copy-start(f32[552]{0:T(1024)S(1)} %broadcast_multiply_fusion.6) | copy-start | bytes 6628
  358.9 112.1 %copy-start.149 = (f32[552]{0:T(1024)}, f32[552]{0:T(1024)S(1)}, u32[]{:S(2)}) copy-start(f32[552]{0:T(1024)S(1)} %fusion.176) | copy-start | bytes 6628
  391.5 49.0 %copy-start.16 = (bf16[4,552,512]{2,1,0:T(8,128)(2,1)S(1)}, bf16[4,552,512]{2,1,0:T(8,128)(2,1)}, u32[]{:S(2)}) copy-start(bf16[4,552,512]{2,1,0:T(8,128)(2,1)} %param.44) | copy-start | bytes 6782980
  477.7 297.5 %all-gather.53.cloned.1.call-start = ((), (), s32[]{:S(2)}) async-start(), calls=%async_computation.19 | async-start | bytes 1695744 | tf_op jit(solution)/shard_map/all_gather | solution.py:340
  478.3 296.9 %all-gather.61.cloned.1.call-start = ((), (), s32[]{:S(2)}) async-start(), calls=%async_computation.28 | async-start | bytes 1695744 | tf_op jit(solution)/shard_map/all_gather | solution.py:341
  479.7 341.0 %all-gather.49.cloned.1.call-start = ((), (), s32[]{:S(2)}) async-start(), calls=%async_computation.17 | async-start | bytes 1695744 | tf_op jit(solution)/shard_map/all_gather | solution.py:340
  480.3 340.4 %all-gather.57.cloned.1.call-start = ((), (), s32[]{:S(2)}) async-start(), calls=%async_computation.26 | async-start | bytes 1695744 | tf_op jit(solution)/shard_map/all_gather | solution.py:341
  481.7 470.8 %all-gather.51.cloned.1.call-start = ((), (), s32[]{:S(2)}) async-start(), calls=%async_computation.18 | async-start | bytes 1695744 | tf_op jit(solution)/shard_map/all_gather | solution.py:340
  482.4 470.1 %all-gather.59.cloned.1.call-start = ((), (), s32[]{:S(2)}) async-start(), calls=%async_computation.27 | async-start | bytes 1695744 | tf_op jit(solution)/shard_map/all_gather | solution.py:341
  514.1 70.0 %copy-start.126 = (f32[2,1,4,552]{3,2,1,0:T(4,128)S(1)}, f32[2,1,4,552]{3,2,1,0:T(4,128)}, u32[]{:S(2)}) copy-start(f32[2,1,4,552]{3,2,1,0:T(4,128)} %copy-done.125) | copy-start | bytes 52996
  595.2 61.6 %copy-start.131 = (f32[2,1,4,552]{3,2,1,0:T(4,128)S(1)}, f32[2,1,4,552]{3,2,1,0:T(4,128)}, u32[]{:S(2)}) copy-start(f32[2,1,4,552]{3,2,1,0:T(4,128)} %copy-done.130) | copy-start | bytes 52996
  667.6 61.9 %copy-start.205 = (f32[552]{0:T(1024)S(1)}, f32[552]{0:T(1024)}, u32[]{:S(2)}) copy-start(f32[552]{0:T(1024)} %get-tuple-element.1836) | copy-start | bytes 6628
  881.8 229.5 %reduce-scatter.10.cloned.1.call-start = ((), (), s32[]{:S(2)}) async-start(), calls=%async_computation.23 | async-start | bytes 1081344 | tf_op jit(solution)/shard_map/reduce_scatter | solution.py:399
  952.4 275.6 %reduce-scatter.6.cloned.1.call-start = ((), (), s32[]{:S(2)}) async-start(), calls=%async_computation.21 | async-start | bytes 2162688 | tf_op jit(solution)/shard_map/reduce_scatter | solution.py:394
  1008.3 324.1 %reduce-scatter.8.cloned.1.call-start = ((), (), s32[]{:S(2)}) async-start(), calls=%async_computation.22 | async-start | bytes 3244032 | tf_op jit(solution)/shard_map/reduce_scatter | solution.py:398
  1019.1 457.9 %reduce-scatter.12.cloned.1.call-start = ((), (), s32[]{:S(2)}) async-start(), calls=%async_computation.24 | async-start | bytes 4325376 | tf_op jit(solution)/shard_map/reduce_scatter | solution.py:403
  1033.1 586.9 %reduce-scatter.14.cloned.1.call-start = ((), (), s32[]{:S(2)}) async-start(), calls=%async_computation.25 | async-start | bytes 4325376 | tf_op jit(solution)/shard_map/reduce_scatter | solution.py:405
  1058.9 48.2 %copy-start.105 = (bf16[552,512]{1,0:T(8,128)(2,1)S(1)}, bf16[552,512]{1,0:T(8,128)(2,1)}, u32[]{:S(2)}) copy-start(bf16[552,512]{1,0:T(8,128)(2,1)} %copy-done.104) | copy-start | bytes 1695748
  (273 other events, 1476.5 us)
Sparse Core Ops, SparseCore 0:
  10.9 56.5 all-gather.24
  70.3 54.1 all-gather.26
  128.4 21.1 all-gather.44
  151.0 23.8 all-gather.46
  176.3 24.9 all-gather.40
  202.7 24.6 all-gather.42
  229.0 22.4 all-gather.36
  253.0 22.1 all-gather.38
  276.8 22.1 all-gather.28
  300.4 22.1 all-gather.30
  325.7 56.4 all-gather.32
  385.2 55.2 all-gather.34
  442.0 21.0 all-gather.54
  477.8 27.6 all-gather.62
  506.9 22.9 all-gather.52
  531.2 22.2 all-gather.60
  554.9 28.2 all-gather.48
  584.5 22.1 all-gather.56
  608.3 22.1 all-gather.50
  881.9 23.5 all-gather.58
  952.5 137.9 reduce-scatter.9
  1093.3 134.5 reduce-scatter.5
  1234.0 98.3 reduce-scatter.7
  1335.1 141.8 reduce-scatter.11
  1479.8 140.0 reduce-scatter.13
where the time goes:
time: 1640 us; the launch traced here: 1630 us
  waiting for transfers between devices  600 us (37%)
  matrix products  473 us (29%)
  local copies, waits for them, and re-layouts  238 us (15%)
  blocking collectives  231 us (14%)
  other arithmetic  41.5 us (3%)
  between operations  23 us (1%)
  loops' own time  19.1 us (1%)
    reduce_scatter x1, waiting for transfers between devices, local(): lax.psum_scatter(totals[9], ('fsdp', 'seq'), scatter_dimension=0, tiled=T...  145 us
    reduce_scatter x1, waiting for transfers between devices, local(): lax.psum_scatter(totals[11], ('fsdp', 'seq'), scatter_dimension=0, tiled=...  143 us
    reduce_scatter x1, waiting for transfers between devices, local(): lax.psum_scatter(totals[0], ('fsdp', 'seq'), scatter_dimension=0, tiled=T...  117 us
    reduce_scatter x1, waiting for transfers between devices, local(): lax.psum_scatter(totals[4], ('fsdp', 'seq'), scatter_dimension=0, tiled=T...  104 us
    dynamic_slice x112, local copies, waits for them, and re-layouts, head_slice(): lax.dynamic_slice_in_dim(array, head_group * group_width, group_width, 2)  83.2 us
    unnamed x2, blocking collectives  83.1 us
    dot_general x24, matrix products, masked_scores(): jnp.einsum('sqhd,skhd->shqk', query_part, key_part, preferred_element_typ...  72.1 us
    dot_general x8, matrix products, one_group(): jnp.einsum('shqk,sqhd->skhd', score_grad, query_part, preferred_element_t...  71 us
  transfers between devices with their start and end apart: 25, of which 8 were waited for; matrix products, arithmetic and copies ran while one was open for 44% of the time, Pallas kernels for 0%

commit v1 on v0

--- a/solution.py
+++ b/solution.py
@@ -1,6 +1,10 @@
+import functools
+
 import jax
 import jax.numpy as jnp
 from jax import lax
+from jax.experimental import pallas as pl
+from jax.experimental.pallas import tpu as pltpu
 from jax.sharding import PartitionSpec as P
 
 HEAD_DIM = 64
@@ -166,7 +170,7 @@
     return (restack(key_grads), restack(value_grads))
 
 
-def local(
+def general(
     inputs,
     skip_input,
     cotangent,
@@ -428,9 +432,407 @@
     )
 
 
+EPS=1e-5
+bf=jnp.bfloat16; f32=jnp.float32
+MASKED=-1e30
+
+def dot_nn(a,b): return lax.dot_general(a,b,(((1,),(0,)),((),())),preferred_element_type=f32)
+def dot_nt(a,b): return lax.dot_general(a,b,(((1,),(1,)),((),())),preferred_element_type=f32)
+def dot_tn(a,b): return lax.dot_general(a,b,(((0,),(0,)),((),())),preferred_element_type=f32)
+
+def lane_iota(shape): return lax.broadcasted_iota(jnp.int32, shape, len(shape)-1)
+def row_iota(shape): return lax.broadcasted_iota(jnp.int32, shape, len(shape)-2)
+
+def norm_parts(h):
+    mu=jnp.mean(h,axis=-1,keepdims=True)
+    c=h-mu
+    var=jnp.mean(c*c,axis=-1,keepdims=True)
+    r=lax.rsqrt(var+EPS)
+    return c*r, r
+
+def attn_fwd_kernel(meta, sf_ref, w_ref, g_ref, b_ref, qkv_ref, e_ref, mix_ref, r_ref, qp, ot, *, L, QP, QB):
+    i=pl.program_id(0)
+    W=128
+    @pl.when(i==0)
+    def _():
+        n,_=norm_parts(sf_ref[...].astype(f32))
+        a=(n*g_ref[...]+b_ref[...]).astype(bf)
+        for j in range(6):
+            t=dot_nn(a,w_ref[:,256*j:256*(j+1)]).astype(bf)
+            qkv_ref[2*j]=t[:,:128]
+            qkv_ref[2*j+1]=t[:,128:]
+        qp[L:,:]=jnp.zeros((QP-L,W),bf)
+    lane=lane_iota((1,W))
+    q=qkv_ref[i].astype(f32)*(HEAD_DIM**-0.5)
+    qp[:L,:]=q.astype(bf)
+    k=qkv_ref[4+i]
+    vt=qkv_ref[8+i].T
+    half=meta[0]; y=meta[1]; limit=meta[2]
+    row=row_iota((L,W))
+    pos=jnp.where(row<half, row+y*half, row-half+(1-y)*half) if True else row
+    bias=jnp.where(pos<limit, 0.0, MASKED).astype(bf)
+    qfull=qp[...]
+    for h in range(2):
+        mine=(lane>=64*h)&(lane<64*h+64)
+        spare=64*(1-h)
+        ka=jnp.where(mine,k,jnp.where(lane==spare,bias,jnp.zeros_like(bias)))
+        qa=jnp.where(lane==spare, jnp.ones_like(qfull), qfull)
+        for j in range(QP//QB):
+            s=dot_nt(ka,qa[j*QB:(j+1)*QB])
+            m=jnp.max(s,axis=0,keepdims=True)
+            e=jnp.exp(s-m)
+            t=jnp.sum(e,axis=0,keepdims=True)
+            el=e.astype(bf)
+            e_ref[h,:,j*QB:(j+1)*QB]=el
+            r=1.0/t
+            r_ref[0,h:h+1,j*QB:(j+1)*QB]=r
+            ot[64*h:64*h+64,j*QB:(j+1)*QB]=dot_nn(vt[64*h:64*h+64],el)*r
+    mix_ref[...]=ot[...].astype(bf).T[:L]
+
+def attn_fwd(meta, sf, w, g, b, *, QB=384):
+    L,D=sf.shape
+    QP=-(-L//128)*128
+    H2=D//128
+    full=lambda *s: pl.BlockSpec(s, lambda i,m:(0,)*len(s))
+    return pl.pallas_call(
+        functools.partial(attn_fwd_kernel,L=L,QP=QP,QB=QB),
+        grid_spec=pltpu.PrefetchScalarGridSpec(num_scalar_prefetch=1, grid=(H2,),
+          in_specs=[full(L,D),full(D,3*D),full(1,D),full(1,D)],
+          out_specs=[full(3*H2,L,128), pl.BlockSpec((2,L,QP),lambda i,m:(i,0,0)), pl.BlockSpec((L,128),lambda i,m:(0,i)), pl.BlockSpec((1,2,QP),lambda i,m:(i,0,0))],
+          scratch_shapes=[pltpu.VMEM((QP,128),bf), pltpu.VMEM((128,QP),f32)]),
+        out_shape=[jax.ShapeDtypeStruct((3*H2,L,128),bf), jax.ShapeDtypeStruct((2*H2,L,QP),bf), jax.ShapeDtypeStruct((L,D),bf), jax.ShapeDtypeStruct((H2,2,QP),f32)],
+        compiler_params=pltpu.CompilerParams(vmem_limit_bytes=60<<20),
+        name="attn_fwd",
+        cost_estimate=pl.CostEstimate(flops=int(2*L*D*3*D+8*4*L*L*256), bytes_accessed=int(20e6), transcendentals=8*L*L),
+    )(meta, sf, w, g, b)
+
+def attn_bwd_kernel(q_ref,k_ref,v_ref,e_ref,o_ref,do_ref,r_ref, sf_ref, gss_ref, w_ref, g_ref, b_ref,
+                    gsf_ref, gw_ref, gg_ref, gb_ref, gq, qp, dop, qt, ds, *, L, QP, QB, H2):
+    i=pl.program_id(0)
+    W=128
+    @pl.when(i==0)
+    def _():
+        qp[L:,:]=jnp.zeros((QP-L,W),bf)
+        dop[L:,:]=jnp.zeros((QP-L,W),f32)
+    lane=lane_iota((1,W))
+    qp[:L,:]=(q_ref[0].astype(f32)*(HEAD_DIM**-0.5)).astype(bf)
+    do=do_ref[...].astype(f32)
+    rt=jnp.concatenate([r_ref[0], jnp.zeros((6,QP),f32)],axis=0).T
+    r0=rt[:L,0:1]; r1=rt[:L,1:2]
+    dop[:L,:]=do*jnp.where(lane<64,r0,r1)
+    dof=dop[...]
+    dob=dof.astype(bf)
+    o=o_ref[...].astype(f32)
+    prod=o*dob[:L].astype(f32)
+    qf=qp[...]
+    k=k_ref[0]; v=v_ref[0]
+    kt=k.T
+    dv=jnp.zeros((L,W),f32); dk=jnp.zeros((L,W),f32)
+    for h in range(2):
+        mine=(lane>=64*h)&(lane<64*h+64)
+        sp=64*(1-h)
+        inner=jnp.sum(jnp.where(mine,prod,0.0),axis=1,keepdims=True)
+        ihi=inner.astype(bf); ilo=(inner-ihi.astype(f32)).astype(bf)
+        ihi=jnp.concatenate([ihi.astype(f32),jnp.zeros((QP-L,1),f32)],axis=0)
+        ilo=jnp.concatenate([ilo.astype(f32),jnp.zeros((QP-L,1),f32)],axis=0)
+        dom=jnp.where(mine,dob,jnp.zeros_like(dob))
+        doa=jnp.where(mine,dob,jnp.where(lane==sp,-ihi,jnp.where(lane==sp+1,-ilo,0.0)).astype(bf))
+        va=jnp.where(mine,v,jnp.where((lane==sp)|(lane==sp+1),jnp.ones_like(v),jnp.zeros_like(v)))
+        dv=dv+dot_nn(e_ref[h],dom)
+        for j in range(QP//QB):
+            dp=dot_nt(va,doa[j*QB:(j+1)*QB])
+            d=(e_ref[h,:,j*QB:(j+1)*QB].astype(f32)*dp).astype(bf)
+            ds[:,j*QB:(j+1)*QB]=d
+            qt[64*h:64*h+64,j*QB:(j+1)*QB]=dot_nn(kt[64*h:64*h+64],d)
+        dk=dk+dot_nn(ds[...],jnp.where(mine,qf,jnp.zeros_like(qf)))
+    gq[i]=(qt[...]*(HEAD_DIM**-0.5)).astype(bf).T[:L]
+    gq[H2+i]=dk.astype(bf)
+    gq[2*H2+i]=dv.astype(bf)
+    @pl.when(i==H2-1)
+    def _():
+        n,r=norm_parts(sf_ref[...].astype(f32))
+        a=(n*g_ref[...]+b_ref[...]).astype(bf)
+        acc=jnp.zeros(n.shape,f32)
+        for j in range(3*H2//2):
+            t=jnp.concatenate([gq[2*j],gq[2*j+1]],axis=1)
+            acc=acc+dot_nt(t,w_ref[:,256*j:256*(j+1)])
+            gw_ref[:,256*j:256*(j+1)]=dot_tn(a,t)
+        gg_ref[...]=jnp.sum(acc*n,axis=0,keepdims=True)
+        gb_ref[...]=jnp.sum(acc,axis=0,keepdims=True)
+        e=acc*g_ref[...]
+        gs=gss_ref[...]+r*(e-jnp.mean(e,axis=1,keepdims=True)-n*jnp.mean(e*n,axis=1,keepdims=True))
+        gsf_ref[...]=gs.astype(bf)
+
+def attn_bwd(qkv,e,mix,dmix,r,sf,gss,w,g,b,*,QB=384):
+    L,D=sf.shape
+    H2=D//128
+    QP=e.shape[2]
+    full=lambda *s: pl.BlockSpec(s, lambda i:(0,)*len(s))
+    col=pl.BlockSpec((L,128),lambda i:(0,i))
+    return pl.pallas_call(
+        functools.partial(attn_bwd_kernel,L=L,QP=QP,QB=QB,H2=H2),
+        grid=(H2,),
+        in_specs=[pl.BlockSpec((1,L,128),lambda i:(i,0,0)),pl.BlockSpec((1,L,128),lambda i:(H2+i,0,0)),pl.BlockSpec((1,L,128),lambda i:(2*H2+i,0,0)),
+          pl.BlockSpec((2,L,QP),lambda i:(i,0,0)), col, col, pl.BlockSpec((1,2,QP),lambda i:(i,0,0)),
+          full(L,D), full(L,D), full(D,3*D), full(1,D), full(1,D)],
+        out_specs=[full(L,D),full(D,3*D),full(1,D),full(1,D)],
+        out_shape=[jax.ShapeDtypeStruct((L,D),bf),jax.ShapeDtypeStruct((D,3*D),f32),jax.ShapeDtypeStruct((1,D),f32),jax.ShapeDtypeStruct((1,D),f32)],
+        scratch_shapes=[pltpu.VMEM((3*H2,L,128),bf),pltpu.VMEM((QP,128),bf),pltpu.VMEM((QP,128),f32),pltpu.VMEM((128,QP),f32),pltpu.VMEM((L,QP),bf)],
+        compiler_params=pltpu.CompilerParams(vmem_limit_bytes=62<<20),
+        name="attn_bwd",
+        cost_estimate=pl.CostEstimate(flops=int(2*2*L*D*3*D+8*8*L*L*256), bytes_accessed=int(30e6), transcendentals=0),
+    )(qkv,qkv,qkv,e,mix,dmix,r,sf,gss,w,g,b)
+
+def gelu_both(v):
+    c=lax.erf(v*(0.5**0.5))
+    cdf=0.5+0.5*c
+    pdf=jnp.exp(-0.5*v*v)*0.3989422804014327
+    return v*cdf, cdf+v*pdf
+
+def mid_kernel(valid_ref, mix_ref, sf_ref, cot_ref, pw, pb, g2, b2, uw, ub, dw, db,
+               out_ref, gmix_ref, gss_ref, gpw_ref, guw_ref, gdw_ref, gpb_ref, gg_ref, gb_ref, gub_ref, gdb_ref,
+               apw, auw, adw, *, T, L, FC):
+    i=pl.program_id(0)
+    @pl.when(i==0)
+    def _():
+        for a in (apw,auw,adw,gpb_ref,gg_ref,gb_ref,gub_ref,gdb_ref):
+            a[...]=jnp.zeros(a.shape,a.dtype)
+    D=mix_ref.shape[1]; F=uw.shape[1]
+    mix=mix_ref[...]
+    ss=sf_ref[...].astype(f32)+dot_nn(mix,pw[...])+pb[...]
+    n,r=norm_parts(ss)
+    mlp=(n*g2[...]+b2[...]).astype(bf)
+    row=row_iota((T,1))+i*T
+    valid=jnp.where(row<L, valid_ref[0], valid_ref[1]).astype(f32)
+    gout=cot_ref[...].astype(f32)*valid
+    gb=gout.astype(bf)
+    gdb_ref[...]+=jnp.sum(gout,axis=0,keepdims=True)
+    branch=jnp.zeros((T,D),f32); gm=jnp.zeros((T,D),f32)
+    for c in range(F//FC):
+        cs=slice(c*FC,(c+1)*FC)
+        hp=dot_nn(mlp,uw[:,cs])+ub[:,cs]
+        act,dact=gelu_both(hp)
+        al=act.astype(bf)
+        branch=branch+dot_nn(al,dw[cs,:])
+        adw[cs,:]+=dot_tn(al,gb)
+        gp=dot_nt(gb,dw[cs,:])*dact
+        gl=gp.astype(bf)
+        gub_ref[:,cs]+=jnp.sum(gl.astype(f32),axis=0,keepdims=True)
+        auw[:,cs]+=dot_tn(mlp,gl)
+        gm=gm+dot_nt(gl,uw[:,cs])
+    out_ref[...]=((ss+branch+db[...])*valid).astype(bf)
+    gg_ref[...]+=jnp.sum(gm*n,axis=0,keepdims=True)
+    gb_ref[...]+=jnp.sum(gm,axis=0,keepdims=True)
+    e=gm*g2[...]
+    gs=gout+r*(e-jnp.mean(e,axis=1,keepdims=True)-n*jnp.mean(e*n,axis=1,keepdims=True))
+    gss_ref[...]=gs
+    gl=gs.astype(bf)
+    gpb_ref[...]+=jnp.sum(gl.astype(f32),axis=0,keepdims=True)
+    apw[...]+=dot_tn(mix,gl)
+    gmix_ref[...]=dot_nt(gl,pw[...]).astype(bf)
+    @pl.when(i==pl.num_programs(0)-1)
+    def _():
+        gpw_ref[...]=apw[...].astype(gpw_ref.dtype)
+        guw_ref[...]=auw[...].astype(guw_ref.dtype)
+        gdw_ref[...]=adw[...].astype(gdw_ref.dtype)
+
+def mid(valid, mix, sf, cot, pw, pb, g2, b2, uw, ub, dw, db, *, L, T, FC=512, gdt=bf):
+    N,D=mix.shape; F=uw.shape[1]
+    tile=pl.BlockSpec((T,D),lambda i,m:(i,0))
+    full=lambda *s: pl.BlockSpec(s, lambda i,m:(0,)*len(s), pipeline_mode=pl.Buffered(1))
+    sd=jax.ShapeDtypeStruct
+    return pl.pallas_call(
+        functools.partial(mid_kernel,T=T,L=L,FC=FC),
+        grid_spec=pltpu.PrefetchScalarGridSpec(num_scalar_prefetch=1,grid=(N//T,),
+          in_specs=[tile,tile,tile,full(D,D),full(1,D),full(1,D),full(1,D),full(D,F),full(1,F),full(F,D),full(1,D)],
+          out_specs=[tile,tile,tile,full(D,D),full(D,F),full(F,D),full(1,D),full(1,D),full(1,D),full(1,F),full(1,D)],
+          scratch_shapes=[pltpu.VMEM((D,D),f32),pltpu.VMEM((D,F),f32),pltpu.VMEM((F,D),f32)]),
+        out_shape=[sd((N,D),bf),sd((N,D),bf),sd((N,D),f32),sd((D,D),gdt),sd((D,F),gdt),sd((F,D),gdt),
+                   sd((1,D),f32),sd((1,D),f32),sd((1,D),f32),sd((1,F),f32),sd((1,D),f32)],
+        compiler_params=pltpu.CompilerParams(vmem_limit_bytes=62<<20),
+        name="mid",
+        cost_estimate=pl.CostEstimate(flops=int(3*2*N*(D*D+2*D*F)), bytes_accessed=int(25e6), transcendentals=2*N*F),
+    )(valid,mix,sf,cot,pw,pb,g2,b2,uw,ub,dw,db)
+
+
+BOTH = ("fsdp", "seq")
+SWAP = ((0, 1), (1, 0))
+
+
+def pack_rows(arrays, width):
+    vectors = jnp.concatenate([a.reshape(-1) for a in arrays if a.ndim == 1])
+    space = (-vectors.shape[0]) % (16 * width)
+    rows = [a.reshape(-1, width) for a in arrays if a.ndim == 2]
+    rows.append(jnp.pad(vectors, (0, space)).reshape(-1, width))
+    return jnp.concatenate(rows, axis=0)
+
+
+def unpack_rows(packed, arrays, width):
+    devices = packed.shape[0]
+    found, at = {}, 0
+    for index, a in enumerate(arrays):
+        if a.ndim == 2:
+            rows = a.size // width
+            piece = packed[:, at : at + rows]
+            found[index] = piece.reshape(devices * a.shape[0], a.shape[1])
+            at += rows
+    vectors = packed[:, at:].reshape(devices, -1)
+    at = 0
+    for index, a in enumerate(arrays):
+        if a.ndim == 1:
+            found[index] = vectors[:, at : at + a.size].reshape(-1)
+            at += a.size
+    return [found[index] for index in range(len(arrays))]
+
+
+def pack_grads(grads, arrays, width):
+    devices = grads[0].shape[0] // arrays[0].shape[0]
+    rows = []
+    for g, a in zip(grads, arrays):
+        if a.ndim == 2:
+            rows.append(g.astype(bf).reshape(devices, -1, width))
+    vectors = jnp.concatenate(
+        [g.reshape(devices, -1) for g, a in zip(grads, arrays) if a.ndim == 1], axis=1
+    ).astype(bf)
+    space = (-vectors.shape[1]) % (16 * width)
+    rows.append(jnp.pad(vectors, ((0, 0), (0, space))).reshape(devices, -1, width))
+    return jnp.concatenate(rows, axis=1)
+
+
+def paired(inputs, skip_input, cotangent, text_len, batch_valid, *params):
+    half, width = inputs.shape[1:]
+    length = 2 * half
+    side = lax.axis_index("seq")
+    held = inputs.shape[0] // 2
+    swap = lambda a: lax.ppermute(a, "seq", SWAP)
+    keep = lambda a: lax.dynamic_slice_in_dim(a, side * held, held, 0)
+    give = lambda a: lax.dynamic_slice_in_dim(a, (1 - side) * held, held, 0)
+
+    packed = pack_rows(params, width)
+    gathered = lax.all_gather(packed, BOTH, axis=0)
+    (
+        skip_matrix,
+        skip_offset,
+        gain_one,
+        shift_one,
+        qkv_matrix,
+        proj_matrix,
+        proj_offset,
+        gain_two,
+        shift_two,
+        up_matrix,
+        up_offset,
+        down_matrix,
+        down_offset,
+    ) = unpack_rows(gathered, params, width)
+    row = lambda v: v.astype(f32)[None, :]
+
+    def first_stream(x, s):
+        return (
+            jnp.dot(x, skip_matrix[:width], preferred_element_type=f32)
+            + jnp.dot(s, skip_matrix[width:], preferred_element_type=f32)
+            + skip_offset.astype(f32)
+        ).astype(bf)
+
+    cot_there = swap(give(cotangent))
+    stream_there = swap(first_stream(give(inputs), give(skip_input)))
+    stream_here = first_stream(keep(inputs), keep(skip_input))
+    stream = jnp.concatenate([stream_here, stream_there], axis=1)
+    cot = jnp.concatenate([keep(cotangent), cot_there], axis=1)
+    lens = keep(text_len)
+    valid = lax.dynamic_slice_in_dim(batch_valid[0], side * held, held, 0)
+
+    fwd = []
+    for s in range(held):
+        meta = jnp.stack([jnp.int32(half), side.astype(jnp.int32), PATCHES + 1 + lens[s]])
+        fwd.append(attn_fwd(meta, stream[s], qkv_matrix, row(gain_one), row(shift_one)))
+    mix = jnp.concatenate([f[2] for f in fwd], axis=0)
+    (
+        out,
+        grad_mix,
+        grad_second,
+        proj_grad,
+        up_grad,
+        down_grad,
+        proj_offset_grad,
+        gain_two_grad,
+        shift_two_grad,
+        up_offset_grad,
+        down_offset_grad,
+    ) = mid(
+        valid,
+        mix,
+        stream.reshape(-1, width),
+        cot.reshape(-1, width),
+        proj_matrix,
+        row(proj_offset),
+        row(gain_two),
+        row(shift_two),
+        up_matrix,
+        row(up_offset),
+        down_matrix,
+        row(down_offset),
+        L=length,
+        T=736,
+    )
+    out = out.reshape(held, length, width)
+    grad_mix = grad_mix.reshape(held, length, width)
+    grad_second = grad_second.reshape(held, length, width)
+    out_there = swap(out[:, half:])
+    bwd = []
+    for s in range(held):
+        qkv, e, m, r = fwd[s]
+        bwd.append(
+            attn_bwd(
+                qkv, e, m, grad_mix[s], r, stream[s], grad_second[s], qkv_matrix, row(gain_one), row(shift_one)
+            )
+        )
+    total = lambda k: functools.reduce(jnp.add, [b[k] for b in bwd])
+    grad_first = jnp.stack([b[0] for b in bwd])
+    first_here = grad_first[:, :half]
+    first_there = swap(grad_first[:, half:])
+
+    def own_order(here, there):
+        low = jnp.where(side == 0, here, there)
+        high = jnp.where(side == 0, there, here)
+        return jnp.concatenate([low, high], axis=0)
+
+    output = own_order(out[:, :half], out_there)
+    first = own_order(first_here, first_there)
+    flat = first.reshape(-1, width)
+    input_grad = dot_nt(flat, skip_matrix[:width]).astype(bf).reshape(inputs.shape)
+    skip_grad = dot_nt(flat, skip_matrix[width:]).astype(bf).reshape(inputs.shape)
+    skip_matrix_grad = jnp.concatenate(
+        [dot_tn(inputs.reshape(-1, width), flat), dot_tn(skip_input.reshape(-1, width), flat)], axis=0
+    )
+    skip_offset_grad = jnp.sum(flat.astype(f32), axis=0)
+    grads = [
+        skip_matrix_grad,
+        skip_offset_grad,
+        total(2)[0],
+        total(3)[0],
+        total(1),
+        proj_grad,
+        proj_offset_grad[0],
+        gain_two_grad[0],
+        shift_two_grad[0],
+        up_grad,
+        up_offset_grad[0],
+        down_grad,
+        down_offset_grad[0],
+    ]
+    scattered = lax.psum_scatter(pack_grads(grads, params, width), BOTH, scatter_dimension=0)
+    own = unpack_rows(scattered[None], params, width)
+    return (output, input_grad, skip_grad, *[g.astype(f32) for g in own])
+
+
+def body_for(mesh):
+    return paired if mesh.shape["seq"] == 2 else general
+
+
 def solution(mesh):
     return jax.shard_map(
-        local,
+        body_for(mesh),
         mesh=mesh,
         in_specs=(
             P("fsdp", "seq", None),

time: 1640 us -> 567 us (0.35)
  matrix products: 473 us -> 16.8 us
  waiting for transfers between devices: 600 us -> 205 us
  blocking collectives: 231 us -> 0 us
  Pallas kernels: 0 us -> 223 us
  local copies, waits for them, and re-layouts: 238 us -> 57 us
  loops' own time: 19.1 us -> 0 us
    dot_general x124 -> x8, matrix products: 473 us -> 16.8 us  [the longest x2 5.5 us: dot_nt(): lax.dot_general(a, b, (((1,), (1,)), ((), ())), preferred_element_type=f32)]
    reduce_scatter x5 -> x1, waiting for transfers between devices: 509 us -> 87.7 us  [paired(): lax.psum_scatter(pack_grads(grads, params, width), BOTH, scatter_dimensio...]
    pallas_call x0 -> x5, Pallas kernels: none -> 223 us  [the longest x2 117 us: attn_bwd(): pl.pallas_call(functools.partial(attn_bwd_kernel, L=L, QP=QP, QB=QB, H2=H...]
    all_gather x9 -> x0, blocking collectives: 148 us -> none  [the longest x1 70.1 us: local(): lax.all_gather(proj_weight, ('fsdp', 'seq'), axis=0, tiled=True)]
    dynamic_slice x168 -> x3, local copies, waits for them, and re-layouts: 102 us -> 2.46 us  [the longest x2 1.88 us: paired(): keep = lambda a: lax.dynamic_slice_in_dim(a, side * held, held, 0)]
    unnamed x2 -> x0, blocking collectives: 83.1 us -> none
    ppermute x0 -> x4, waiting for transfers between devices: none -> 70.7 us  [paired(): swap = lambda a: lax.ppermute(a, 'seq', SWAP)]
    unnamed x548 -> x65, local copies, waits for them, and re-layouts: 59 us -> 11 us
  transfers between devices with their start and end apart: 25 -> 6, of which waited for: 8 -> 6; matrix products, arithmetic and copies ran while one was open for 44% -> 7% of each run, Pallas kernels for 0% -> 0%
where the time goes in v1:
time: 567 us; the launch traced here: 557 us
  Pallas kernels  223 us (39%)
  waiting for transfers between devices  205 us (36%)
  local copies, waits for them, and re-layouts  57 us (10%)
  other arithmetic  31.6 us (6%)
  matrix products  16.8 us (3%)
  between operations  16.1 us (3%)
  starting transfers between devices  7.62 us (1%)
    pallas_call x2, Pallas kernels, attn_bwd(): pl.pallas_call(functools.partial(attn_bwd_kernel, L=L, QP=QP, QB=QB, H2=H...  117 us
    reduce_scatter x1, waiting for transfers between devices, paired(): lax.psum_scatter(pack_grads(grads, params, width), BOTH, scatter_dimensio...  87.7 us
    ppermute x4, waiting for transfers between devices, paired(): swap = lambda a: lax.ppermute(a, 'seq', SWAP)  70.7 us
    pallas_call x2, Pallas kernels, attn_fwd(): pl.pallas_call(functools.partial(attn_fwd_kernel, L=L, QP=QP, QB=QB), gri...  57.7 us
    pallas_call x1, Pallas kernels, mid(): pl.pallas_call(functools.partial(mid_kernel, T=T, L=L, FC=FC), grid_spec=...  48.4 us
    all_gather x1, waiting for transfers between devices, paired(): gathered = lax.all_gather(packed, BOTH, axis=0)  46.3 us
  transfers between devices with their start and end apart: 6, of which 6 were waited for; matrix products, arithmetic and copies ran while one was open for 7% of the time, Pallas kernels for 0%

profile of v1, /device:TPU:0, one launch (start us, length us, event | category | flops | bytes accessed | tf_op | source)
XLA Modules:
  0.0 556.8 jit_solution(13448549215522195818)
XLA Ops:
  7.2 5.4 concatenate.32
  17.6 1.8 constant_dynamic-slice_fusion.1
  19.4 3.1 collective-permute-start.1
  25.6 23.6 %collective-permute-done.1 = bf16[2,552,512]{2,1,0:T(8,128)(2,1)S(1)} collective-permute-done((bf16[2,552,512]{2,1,0:T(8,128)(2,1)S(1)}, bf16[2,552,512]{2,1,0:T(8,128)(2,1)S(1)}, u32[]{:S(2)}, u32[]{:S(2)}) %collective-permute-start.1) | collective-permute-done | bytes 1130528 | tf_op jit(solution)/shard_map/ppermute | solution.py:707
  49.2 1.5 pad_maximum_fusion.2
  50.7 46.3 %all-gather.3.cloned.1.call-done = bf16[7680,512]{1,0:T(8,128)(2,1)} async-done(((bf16[240,512]{1,0:T(8,128)(2,1)}), bf16[7680,512]{1,0:T(8,128)(2,1)}) %all-gather.3.cloned.1.call-update) | async-done | bytes 7864336 | tf_op jit(solution)/shard_map/all_gather | solution.py:712
  97.0 2.1 fusion.35
  99.1 2.1 fusion.34
  101.1 1.5 slice.191
  103.1 2.1 fusion.10
  105.3 1.8 add_convert_fusion.1
  107.1 1.5 collective-permute-start
  113.3 1.7 reshape.263.w_ref
  114.9 3.9 fusion.33
  118.9 2.6 reshape.267.uw
  121.4 2.1 fusion.13
  124.4 10.1 %collective-permute-done = bf16[2,552,512]{2,1,0:T(8,128)(2,1)} collective-permute-done((bf16[2,552,512]{2,1,0:T(8,128)(2,1)}, bf16[2,552,512]{2,1,0:T(8,128)(2,1)}, u32[]{:S(2)}, u32[]{:S(2)}) %collective-permute-start) | collective-permute-done | bytes 1130528 | tf_op jit(solution)/shard_map/ppermute | solution.py:707
  134.5 2.7 fusion.6
  137.2 28.7 %attn_fwd.2 = (bf16[12,1104,128]{2,1,0:T(8,128)(2,1)}, bf16[8,1104,1152]{2,1,0:T(8,128)(2,1)}, bf16[1104,512]{1,0:T(8,128)(2,1)}, f32[4,2,1152]{2,1,0:T(2,128)}) custom-call(s32[3]{0:T(128)} %get-tuple-element.112.meta, bf16[1104,512]{1,0:T(8,128)(2,1)} %get-tuple-element.90.sf_ref, bf16[512,1536]{1,0:T(8,128)(2,1)} %reshape.263.w_ref, ...), custom_call_target="tpu_custom_call" | custom-call | flops 11720982528 | bytes 20000000 | tf_op jit(solution)/shard_map/attn_fwd/pallas_call | solution.py:497
  165.9 29.0 %attn_fwd.3 = (bf16[12,1104,128]{2,1,0:T(8,128)(2,1)}, bf16[8,1104,1152]{2,1,0:T(8,128)(2,1)}, bf16[1104,512]{1,0:T(8,128)(2,1)}, f32[4,2,1152]{2,1,0:T(2,128)}) custom-call(s32[3]{0:T(128)} %get-tuple-element.113.meta, bf16[1104,512]{1,0:T(8,128)(2,1)} %get-tuple-element.91.sf_ref, bf16[512,1536]{1,0:T(8,128)(2,1)} %reshape.263.w_ref, ...), custom_call_target="tpu_custom_call" | custom-call | flops 11720982528 | bytes 20000000 | tf_op jit(solution)/shard_map/attn_fwd/pallas_call | solution.py:497
  194.9 2.8 pad_maximum_fusion.1.mix_ref
  197.7 2.8 pad_maximum_fusion
  200.4 48.4 %mid.1 = (bf16[2208,512]{1,0:T(8,128)(2,1)}, bf16[2208,512]{1,0:T(8,128)(2,1)}, f32[2208,512]{1,0:T(8,128)}, bf16[512,512]{1,0:T(8,128)(2,1)}, bf16[512,2048]{1,...) custom-call(s32[2]{0:T(128)} %fusion.22.valid_ref, ...), custom_call_target="tpu_custom_call" | custom-call | flops 31255953408 | bytes 25000000 | tf_op jit(solution)/shard_map/mid/pallas_call | solution.py:644
  251.2 3.3 fusion.37
  254.5 2.6 fusion.36
  257.1 58.2 %attn_bwd.3 = (bf16[1104,512]{1,0:T(8,128)(2,1)}, f32[512,1536]{1,0:T(8,128)}, f32[1,512]{1,0:T(1,128)}, f32[1,512]{1,0:T(1,128)}) custom-call(bf16[12,1104,128]{2,1,0:T(8,128)(2,1)} %get-tuple-element.52.q_ref.k_ref.v_ref, bf16[12,1104,128]{2,1,0:T(8,128)(2,1)} %get-tuple-element.52.q_ref.k_ref.v_ref, ...), custom_call_target="tpu_custom_call" | custom-call | flops 23441965056 | bytes 30000000 | tf_op jit(solution)/shard_map/attn_bwd/pallas_call | solution.py:572
  315.3 58.6 %attn_bwd.2 = (bf16[1104,512]{1,0:T(8,128)(2,1)}, f32[512,1536]{1,0:T(8,128)}, f32[1,512]{1,0:T(1,128)}, f32[1,512]{1,0:T(1,128)}) custom-call(bf16[12,1104,128]{2,1,0:T(8,128)(2,1)} %get-tuple-element.46.q_ref.k_ref.v_ref, bf16[12,1104,128]{2,1,0:T(8,128)(2,1)} %get-tuple-element.46.q_ref.k_ref.v_ref, ...), custom_call_target="tpu_custom_call" | custom-call | flops 23441965056 | bytes 30000000 | tf_op jit(solution)/shard_map/attn_bwd/pallas_call | solution.py:572
  373.9 2.3 pad_maximum_fusion.5
  376.2 1.5 collective-permute-start.3
  377.9 3.1 reshape.275
  381.0 4.4 add_convert_fusion
  385.5 3.7 reshape.273
  389.4 13.3 %collective-permute-done.3 = bf16[2,552,512]{2,1,0:T(8,128)(2,1)} collective-permute-done((bf16[2,552,512]{2,1,0:T(8,128)(2,1)}, bf16[2,552,512]{2,1,0:T(8,128)(2,1)}, u32[]{:S(2)}, u32[]{:S(2)}) %collective-permute-start.3) | collective-permute-done | bytes 1130528 | tf_op jit(solution)/shard_map/ppermute | solution.py:707
  402.7 2.6 fusion.32
  405.3 2.2 fusion.2
  407.8 2.3 fusion.3
  410.5 1.4 pad_maximum_fusion.6
  415.1 1.5 constant_dynamic-update-slice_fusion.8
  417.5 1.6 constant_dynamic-update-slice_fusion.7
  420.0 1.5 slice.205
  421.4 1.5 collective-permute-start.2
  423.2 23.7 %collective-permute-done.2 = bf16[2,552,512]{2,1,0:T(8,128)(2,1)S(1)} collective-permute-done((bf16[2,552,512]{2,1,0:T(8,128)(2,1)S(1)}, bf16[2,552,512]{2,1,0:T(8,128)(2,1)S(1)}, u32[]{:S(2)}, u32[]{:S(2)}) %collective-permute-start.2) | collective-permute-done | bytes 1130528 | tf_op jit(solution)/shard_map/ppermute | solution.py:707
  447.0 1.6 pad_maximum_fusion.3
  448.6 2.8 convolution_convert_fusion
  451.4 2.8 convolution_convert_fusion.1
  454.1 87.7 %reduce-scatter.2.cloned.1.call-done = bf16[1,240,512]{2,1,0:T(8,128)(2,1)} async-done(((bf16[32,240,512]{2,1,0:T(8,128)(2,1)}), bf16[1,240,512]{2,1,0:T(8,128)(2,1)}) %reduce-scatter.2.cloned.1.call-update) | async-done | bytes 245776 | tf_op jit(solution)/shard_map/reduce_scatter | solution.py:824
  545.9 1.6 fusion.15
  548.2 1.4 fusion.16
  (114 shorter events, 26.3 us)
Async XLA Ops:
  7.2 17.2 %copy-start = (s32[1,4]{1,0:T(1,128)S(1)}, s32[1,4]{1,0:T(1,128)}, u32[]{:S(2)}) copy-start(s32[1,4]{1,0:T(1,128)} %param.22) | copy-start | bytes 52
  7.2 89.8 %all-gather.3.cloned.1.call-start = ((), (), s32[]{:S(2)}) async-start(), calls=%async_computation.2 | async-start | bytes 8110080 | tf_op jit(solution)/shard_map/all_gather | solution.py:712
  16.8 0.7 copy-start.15
  17.5 524.3 %reduce-scatter.2.cloned.1.call-start = ((), (), s32[]{:S(2)}) async-start(), calls=%async_computation.1 | async-start | bytes 8110080 | tf_op jit(solution)/shard_map/reduce_scatter | solution.py:824
  17.6 4.9 copy-start.25
  19.4 29.8 %collective-permute-start.1 = (bf16[2,552,512]{2,1,0:T(8,128)(2,1)S(1)}, bf16[2,552,512]{2,1,0:T(8,128)(2,1)S(1)}, u32[]{:S(2)}, u32[]{:S(2)}) collective-permute-start(bf16[2,552,512]{2,1,0:T(8,128)(2,1)S(1)} %get-tuple-element.89), channel_id=1, source_target_pairs={{0,1},{1,0},{2,3},{3,2},{4,5},{5,4},{6,7},{7,6},{8,9},{9,8},{10,11... | collective-permute-start | bytes 3391496 | tf_op jit(solution)/shard_map/ppermute | solution.py:707
  103.0 2.3 copy-start.13
  103.1 2.2 copy-start.22
  107.1 27.4 %collective-permute-start = (bf16[2,552,512]{2,1,0:T(8,128)(2,1)}, bf16[2,552,512]{2,1,0:T(8,128)(2,1)}, u32[]{:S(2)}, u32[]{:S(2)}) collective-permute-start(bf16[2,552,512]{2,1,0:T(8,128)(2,1)} %add_convert_fusion.1), channel_id=1, source_target_pairs={{0,1},{1,0},{2,3},{3,2},{4,5},{5,4},{6,7},{7,6},{8,9},{9,8},{10,11... | collective-permute-start | bytes 3391496 | tf_op jit(solution)/shard_map/ppermute | solution.py:707
  121.4 2.2 copy-start.14
  121.4 2.2 copy-start.23
  165.9 29.0 %copy-start.11 = (bf16[1104,512]{1,0:T(8,128)(2,1)S(1)}, bf16[1104,512]{1,0:T(8,128)(2,1)}, u32[]{:S(2)}) copy-start(bf16[1104,512]{1,0:T(8,128)(2,1)} %get-tuple-element.43.o_ref) | copy-start | bytes 3391492
  251.2 3.3 copy-start.3
  373.9 3.8 copy-start.17
  373.9 3.9 copy-start.16
  376.2 26.5 %collective-permute-start.3 = (bf16[2,552,512]{2,1,0:T(8,128)(2,1)}, bf16[2,552,512]{2,1,0:T(8,128)(2,1)}, u32[]{:S(2)}, u32[]{:S(2)}) collective-permute-start(bf16[2,552,512]{2,1,0:T(8,128)(2,1)} %pad_maximum_fusion.5), channel_id=1, source_target_pairs={{0,1},{1,0},{2,3},{3,2},{4,5},{5,4},{6,7},{7,6},{8,9},{9,8},{10,11... | collective-permute-start | bytes 3391496 | tf_op jit(solution)/shard_map/ppermute | solution.py:707
  385.4 3.7 copy-start.19
  385.5 3.7 copy-start.21
  385.5 3.9 copy-start.18
  385.5 3.9 copy-start.20
  389.4 15.9 %copy-start.24 = (bf16[4,552,512]{2,1,0:T(8,128)(2,1)S(1)}, bf16[4,552,512]{2,1,0:T(8,128)(2,1)}, u32[]{:S(2)}) copy-start(bf16[4,552,512]{2,1,0:T(8,128)(2,1)} %param.19) | copy-start | bytes 6782980
  405.3 2.3 copy-start.4
  405.3 2.3 copy-start.6
  405.3 2.5 copy-start.9
  410.5 2.5 copy-start.2
  411.9 2.4 copy-start.12
  415.1 2.3 copy-start.10
  419.9 3.1 copy-start.5
  419.9 3.0 copy-start.7
  421.4 25.4 %copy-start.8 = (bf16[2208,512]{1,0:T(8,128)(2,1)S(1)}, bf16[2208,512]{1,0:T(8,128)(2,1)}, u32[]{:S(2)}) copy-start(bf16[2208,512]{1,0:T(8,128)(2,1)} %get-tuple-element.45) | copy-start | bytes 6782980
  421.4 25.4 %collective-permute-start.2 = (bf16[2,552,512]{2,1,0:T(8,128)(2,1)S(1)}, bf16[2,552,512]{2,1,0:T(8,128)(2,1)S(1)}, u32[]{:S(2)}, u32[]{:S(2)}) collective-permute-start(bf16[2,552,512]{2,1,0:T(8,128)(2,1)S(1)} %slice.205), channel_id=1, source_target_pairs={{0,1},{1,0},{2,3},{3,2},{4,5},{5,4},{6,7},{7,6},{8,9},{9,8},{10,11... | collective-permute-start | bytes 3391496 | tf_op jit(solution)/shard_map/ppermute | solution.py:707
  451.4 98.2 %copy-start.1 = (s32[1,4]{1,0:T(1,128)S(1)}, s32[1,4]{1,0:T(1,128)}, u32[]{:S(2)}) copy-start(s32[1,4]{1,0:T(1,128)} %param.22) | copy-start | bytes 52
Sparse Core Ops, SparseCore 0:
  17.6 79.3 all-gather.2
  420.1 121.7 reduce-scatter.1
